TPU v7x, 256 devices: a whole 4x4x8 slice. The times are simulated.
256 devices in a mesh: pair: 4 (over y_hi, core), cd: 64 (over z, x, y_lo).
Axes of the slice: x: 4, y: 4 (y_hi: 2, y_lo: 2; y = y_hi * 2 + y_lo), z: 8, core: 2. Of those that a mesh axis runs over, the one named last changes fastest.
Arguments:
- lambda_amps: bfloat16 [11264, 1024], P('pair'), may hold values from -0.0546875 to 0.0546875
- t_amps: bfloat16 [11264, 1024], P('pair', 'cd'), may hold values from -6 to 6
- coef_mu: float32 [768, 64], P('pair'), may hold values from -0.75 to 0.75
- coef_nu: float32 [768, 16], replicated, may hold values from -1.5 to 1.5
Outputs:
- half_ao: bfloat16 [768, 768, 1024], P('pair', 'cd')
All inputs are finite; a program needn't handle non-finite values.
Results may differ from a plain program's by a relative error of at most 0.001.
Values sent between devices are 32-bit elements; how exact they have to be, the bound alone decides.
A program may use at most 64 MiB of HBM per device.

v0:
```python
import jax
import jax.numpy as jnp
from jax import lax
from jax.sharding import PartitionSpec as P

A = 64
B = 16


def cut_along(array, dim, peers):
    before, after = (array.shape[:dim], array.shape[dim + 1 :])
    return jnp.moveaxis(array.reshape(*before, peers, -1, *after), dim, 0)


def sent_and_summed(array, axis, dim):
    blocks = cut_along(array, dim, lax.axis_size(axis))
    arrived = lax.all_to_all(blocks, axis, split_axis=0, concat_axis=0, tiled=True)
    return arrived.sum(axis=0)


def body(lambda_amps, t_amps, coef_mu, coef_nu):
    partial_value = lax.dot_general(
        lambda_amps, t_amps, (((0,), (0,)), ((), ())), preferred_element_type=jnp.float32
    )
    local_cols = partial_value.shape[1]
    groups = lax.axis_size("pair")
    share = sent_and_summed(partial_value.reshape(A, B * local_cols), "pair", 0)
    panel = share.reshape(A // groups, B, local_cols)
    half = jnp.einsum("abc,nb->nac", panel, coef_nu, precision=lax.Precision.HIGHEST)
    moved = lax.all_to_all(half, "cd", split_axis=0, concat_axis=2, tiled=True)
    gathered = lax.all_gather(moved, "pair", axis=1, tiled=True)
    result = jnp.einsum("ma,nac->mnc", coef_mu, gathered, precision=lax.Precision.HIGHEST)
    return result.astype(jnp.bfloat16)


def solution(mesh):
    in_specs = (P("pair", None), P("pair", "cd"), P("pair", None), P())
    out_specs = P("pair", "cd", None)
    return jax.shard_map(body, mesh=mesh, in_specs=in_specs, out_specs=out_specs, check_vma=False)
```

profile of v0, /device:TPU:1, one launch (start us, length us, event | category | flops | bytes accessed | tf_op | source)
XLA Modules:
  0.0 139.2 jit_solution(14465179184034495695)
XLA Ops:
  6.5 0.0 copy-start
  6.5 0.0 copy-start.2
  6.5 0.0 all-gather.2.cloned.1.call-start
  6.5 0.9 copy-done
  7.4 4.3 %fusion.2 = f32[1024,16]{1,0:T(8,128)S(1)} fusion(bf16[2816,1024]{1,0:T(8,128)(2,1)} %param.4, bf16[2816,16]{0,1:T(8,128)(2,1)S(1)} %copy-done), kind=kOutput, calls=%fused_computation.4 | convolution fusion | flops 92274688 | bytes 5922816 | tf_op jit(solution)/shard_map/dot_general | solution.py:22
  11.8 0.2 reshape_reshape.3
  12.0 10.5 %all_to_all.23 = f32[4,16,256]{2,1,0:T(8,128)S(1)} all-to-all(f32[4,16,256]{2,1,0:T(8,128)S(1)} %reshape_reshape.3), channel_id=1, replica_groups=mesh['pair'=4,'cd'=64] {'pair'}, dimensions={0} | all-to-all | bytes 131072 | tf_op jit(solution)/shard_map/all_to_all | solution.py:17
  22.5 0.1 reshape.3
  22.6 0.0 copy-done.2
  22.6 0.8 convolution_bitcast_fusion
  23.5 5.0 %copy.11 = f32[768,16,16]{2,1,0:T(8,128)} copy(f32[768,16,16]{0,2,1:T(8,128)S(1)} %convolution_bitcast_fusion) | data formatting | bytes 1572864 | tf_op jit(solution)/shard_map/abc,nb->nac/dot_general | solution.py:29
  28.5 4.8 %reshape.6 = f32[64,1,3072]{2,1,0:T(1,128)S(1)} reshape(f32[768,16,16]{2,1,0:T(8,128)} %copy.11) | data formatting | bytes 1572864
  33.2 32.1 %all_to_all.24 = f32[64,1,3072]{2,1,0:T(1,128)S(1)} all-to-all(f32[64,1,3072]{2,1,0:T(1,128)S(1)} %reshape.6), channel_id=1, replica_groups=mesh['pair'=4,'cd'=64] {'cd'}, dimensions={0} | all-to-all | bytes 1572864 | tf_op jit(solution)/shard_map/all_to_all | solution.py:30
  65.3 0.5 broadcast
  65.8 2.6 %reduce = f32[64,3072]{1,0:T(8,128)S(1)} reduce(f32[64,1,3072]{2,1,0:T(1,128)S(1)} %all_to_all.24, f32[]{:T(128)} %broadcast), dimensions={1}, to_apply=%all_to_all.17.reduce_sub_computation | reduce | bytes 1572868 | tf_op jit(solution)/shard_map/all_to_all | solution.py:30
  68.5 3.8 %reshape.7 = f32[768,16,16]{2,1,0:T(8,128)} reshape(f32[64,3072]{1,0:T(8,128)S(1)} %reduce) | data formatting | bytes 1572864
  72.3 9.1 %copy.13 = f32[12,16,64,16]{3,2,1,0:T(8,128)} copy(f32[12,16,64,16]{3,1,0,2:T(8,128)} %bitcast.20) | data formatting | bytes 1572864 | tf_op jit(solution)/shard_map/all_to_all | solution.py:30
  81.4 0.0 copy-start.1
  81.4 7.1 %all_to_all.20 = f32[12,16,1024]{2,1,0:T(8,128)} reshape(f32[12,16,64,16]{3,2,1,0:T(8,128)} %copy.13) | data formatting | bytes 1572864 | tf_op jit(solution)/shard_map/all_to_all | solution.py:30
  88.5 0.0 all-gather.2.cloned.1.call-update
  88.5 33.2 %all-gather.2.cloned.1.call-done = f32[12,64,1024]{2,1,0:T(8,128)} async-done(((f32[12,16,1024]{2,1,0:T(8,128)}), f32[12,64,1024]{2,1,0:T(8,128)}) %all-gather.2.cloned.1.call-update) | async-done | bytes 3145744 | tf_op jit(solution)/shard_map/all_gather | solution.py:31
  121.7 0.0 copy-done.1
  121.7 10.6 %convert_bitcast_fusion = bf16[192,12,1024]{2,0,1:T(8,128)(2,1)} fusion(f32[12,64,1024]{2,1,0:T(8,128)} %all-gather.2.cloned.1.call-done, f32[192,64]{0,1:T(8,128)S(1)} %copy-done.1), kind=kOutput, calls=%fused_computation | convolution fusion | flops 1814298624 | bytes 7913472 | tf_op jit(solution)/shard_map/ma,nac->mnc/dot_general | solution.py:32
  (1 shorter events, 0.0 us)
Async XLA Ops:
  6.5 0.9 copy-start
  6.5 16.1 %copy-start.2 = (f32[768,16]{0,1:T(8,128)S(1)}, f32[768,16]{0,1:T(8,128)}, u32[]{:S(2)}) copy-start(f32[768,16]{0,1:T(8,128)} %param.7) | copy-start | bytes 147460
  6.5 115.2 %all-gather.2.cloned.1.call-start = ((), (), s32[]{:S(2)}) async-start(), calls=%async_computation.2 | async-start | bytes 3932160 | tf_op jit(solution)/shard_map/all_gather | solution.py:31
  81.4 40.3 %copy-start.1 = (f32[192,64]{0,1:T(8,128)S(1)}, f32[192,64]{0,1:T(8,128)}, u32[]{:S(2)}) copy-start(f32[192,64]{0,1:T(8,128)} %param.6) | copy-start | bytes 147460
Sparse Core Ops, SparseCore 0:
  88.7 33.0 all-gather.1
where the time goes:
time: 140 us; the launch traced here: 139 us
  blocking collectives  42.6 us (30%)
  waiting for transfers between devices  33.2 us (24%)
  local copies, waits for them, and re-layouts  31.5 us (22%)
  matrix products  15.8 us (11%)
  between operations  13.4 us (10%)
  other arithmetic  2.61 us (2%)
    all_gather x1, waiting for transfers between devices, body(): gathered = lax.all_gather(moved, 'pair', axis=1, tiled=True)  33.2 us
    all_to_all x1, blocking collectives, body(): moved = lax.all_to_all(half, 'cd', split_axis=0, concat_axis=2, tiled=True)  32.1 us
    all_to_all x3, local copies, waits for them, and re-layouts, body(): moved = lax.all_to_all(half, 'cd', split_axis=0, concat_axis=2, tiled=True)  16.7 us
    dot_general x1, matrix products, body(): jnp.einsum('ma,nac->mnc', coef_mu, gathered, precision=lax.Precision.HIGH...  10.6 us
    all_to_all x1, blocking collectives, sent_and_summed(): lax.all_to_all(blocks, axis, split_axis=0, concat_axis=0, tiled=True)  10.5 us
    unnamed x8, local copies, waits for them, and re-layouts  9.51 us
    dot_general x1, local copies, waits for them, and re-layouts, body(): jnp.einsum('abc,nb->nac', panel, coef_nu, precision=lax.Precision.HIGHEST)  4.98 us
    dot_general x1, matrix products, body(): lax.dot_general(lambda_amps, t_amps, (((0,), (0,)), ((), ())), preferred_...  4.33 us
  transfers between devices with their start and end apart: 1, of which 1 were waited for; matrix products, arithmetic and copies ran while one was open for 0% of the time, Pallas kernels for 0%

commit v1 on v0

--- a/solution.py
+++ b/solution.py
@@ -5,6 +5,13 @@
 
 A = 64
 B = 16
+
+
+def gather_over(x, axis, dim):
+    size = lax.axis_size(axis)
+    tiles = jnp.stack([x for _ in range(size)])
+    tiles = lax.all_to_all(tiles, axis, split_axis=0, concat_axis=0)
+    return jnp.concatenate(tiles, axis=dim)
 
 
 def cut_along(array, dim, peers):
@@ -28,7 +35,7 @@
     panel = share.reshape(A // groups, B, local_cols)
     half = jnp.einsum("abc,nb->nac", panel, coef_nu, precision=lax.Precision.HIGHEST)
     moved = lax.all_to_all(half, "cd", split_axis=0, concat_axis=2, tiled=True)
-    gathered = lax.all_gather(moved, "pair", axis=1, tiled=True)
+    gathered = gather_over(moved, "pair", 1)
     result = jnp.einsum("ma,nac->mnc", coef_mu, gathered, precision=lax.Precision.HIGHEST)
     return result.astype(jnp.bfloat16)
 

time: 140 us -> 135 us (0.964)
  blocking collectives: 42.6 us -> 86.2 us
  waiting for transfers between devices: 33.2 us -> 0 us
  between operations: 13.4 us -> 0.08 us
    all_to_all x0 -> x1, blocking collectives: none -> 43.6 us  [gather_over(): tiles = lax.all_to_all(tiles, axis, split_axis=0, concat_axis=0)]
    all_gather x1 -> x0, waiting for transfers between devices: 33.2 us -> none  [body(): gathered = lax.all_gather(moved, 'pair', axis=1, tiled=True)]
    all_to_all x3 -> x2, local copies, waits for them, and re-layouts: 16.7 us -> 9.59 us  [body(): moved = lax.all_to_all(half, 'cd', split_axis=0, concat_axis=2, tiled=True)]
    another operation x0 -> x2, local copies, waits for them, and re-layouts: none -> 6.66 us  [gather_over(): tiles = jnp.stack([x for _ in range(size)])]
  transfers between devices with their start and end apart: 1 -> 0, of which waited for: 1 -> 0; matrix products, arithmetic and copies ran while one was open for 0% -> 0% of each run, Pallas kernels for 0% -> 0%
where the time goes in v1:
time: 135 us
  blocking collectives  86.2 us (64%)
  local copies, waits for them, and re-layouts  31.5 us (23%)
  matrix products  14.5 us (11%)
  other arithmetic  2.61 us (2%)
    all_to_all x1, blocking collectives, gather_over(): tiles = lax.all_to_all(tiles, axis, split_axis=0, concat_axis=0)  43.6 us
    all_to_all x1, blocking collectives, body(): moved = lax.all_to_all(half, 'cd', split_axis=0, concat_axis=2, tiled=True)  32.1 us
    all_to_all x1, blocking collectives, sent_and_summed(): lax.all_to_all(blocks, axis, split_axis=0, concat_axis=0, tiled=True)  10.5 us
    all_to_all x2, local copies, waits for them, and re-layouts, body(): moved = lax.all_to_all(half, 'cd', split_axis=0, concat_axis=2, tiled=True)  9.59 us
    unnamed x8, local copies, waits for them, and re-layouts  9.52 us
    dot_general x1, matrix products, body(): jnp.einsum('ma,nac->mnc', coef_mu, gathered, precision=lax.Precision.HIGH...  9.32 us
    another operation x2, local copies, waits for them, and re-layouts, gather_over(): tiles = jnp.stack([x for _ in range(size)])  6.66 us
    dot_general x1, local copies, waits for them, and re-layouts, body(): jnp.einsum('abc,nb->nac', panel, coef_nu, precision=lax.Precision.HIGHEST)  4.99 us

profile of v1, /device:TPU:1, one launch (start us, length us, event | category | flops | bytes accessed | tf_op | source)
XLA Modules:
  0.0 134.9 jit_solution(1001069900202482397)
XLA Ops:
  0.0 0.0 copy-start
  0.0 0.0 copy-start.2
  0.0 0.9 copy-done
  0.9 4.3 %fusion.2 = f32[1024,16]{1,0:T(8,128)S(1)} fusion(bf16[2816,1024]{1,0:T(8,128)(2,1)} %param.4, bf16[2816,16]{0,1:T(8,128)(2,1)S(1)} %copy-done), kind=kOutput, calls=%fused_computation.4 | convolution fusion | flops 92274688 | bytes 5922816 | tf_op jit(solution)/shard_map/dot_general | solution.py:29
  5.2 0.2 reshape_reshape.3
  5.5 10.5 %all_to_all.25 = f32[4,16,256]{2,1,0:T(8,128)S(1)} all-to-all(f32[4,16,256]{2,1,0:T(8,128)S(1)} %reshape_reshape.3), channel_id=1, replica_groups=mesh['pair'=4,'cd'=64] {'pair'}, dimensions={0} | all-to-all | bytes 131072 | tf_op jit(solution)/shard_map/all_to_all | solution.py:24
  16.0 0.1 reshape.12
  16.1 0.0 copy-done.2
  16.1 0.8 convolution_bitcast_fusion
  16.9 5.0 %copy.10 = f32[768,16,16]{2,1,0:T(8,128)} copy(f32[768,16,16]{0,2,1:T(8,128)S(1)} %convolution_bitcast_fusion) | data formatting | bytes 1572864 | tf_op jit(solution)/shard_map/abc,nb->nac/dot_general | solution.py:36
  21.9 4.8 %reshape.17 = f32[64,1,3072]{2,1,0:T(1,128)S(1)} reshape(f32[768,16,16]{2,1,0:T(8,128)} %copy.10) | data formatting | bytes 1572864
  26.7 32.1 %all_to_all.26 = f32[64,1,3072]{2,1,0:T(1,128)S(1)} all-to-all(f32[64,1,3072]{2,1,0:T(1,128)S(1)} %reshape.17), channel_id=1, replica_groups=mesh['pair'=4,'cd'=64] {'cd'}, dimensions={0} | all-to-all | bytes 1572864 | tf_op jit(solution)/shard_map/all_to_all | solution.py:37
  58.8 0.5 broadcast.1
  59.3 2.6 %reduce = f32[64,3072]{1,0:T(8,128)S(1)} reduce(f32[64,1,3072]{2,1,0:T(1,128)S(1)} %all_to_all.26, f32[]{:T(128)} %broadcast.1), dimensions={1}, to_apply=%all_to_all.18.reduce_sub_computation | reduce | bytes 1572868 | tf_op jit(solution)/shard_map/all_to_all | solution.py:37
  61.9 3.8 %reshape.18 = f32[768,16,16]{2,1,0:T(8,128)} reshape(f32[64,3072]{1,0:T(8,128)S(1)} %reduce) | data formatting | bytes 1572864
  65.8 9.1 %copy.12 = f32[12,16,64,16]{3,2,1,0:T(8,128)} copy(f32[12,16,64,16]{3,1,0,2:T(8,128)} %bitcast.22) | data formatting | bytes 1572864 | tf_op jit(solution)/shard_map/all_to_all | solution.py:37
  74.9 6.3 %stack.4 = f32[12,16,1024]{2,1,0:T(8,128)S(1)} reshape(f32[12,16,64,16]{3,2,1,0:T(8,128)} %copy.12) | data formatting | bytes 1572864 | tf_op jit(solution)/shard_map/stack | solution.py:12
  81.1 0.4 stack.10
  81.5 0.0 copy-start.1
  81.5 43.6 %all_to_all.27 = f32[4,12,16,1024]{3,2,1,0:T(8,128)S(1)} all-to-all(f32[4,12,16,1024]{3,2,1,0:T(8,128)S(1)} %stack.10), channel_id=1, replica_groups=mesh['pair'=4,'cd'=64] {'pair'}, dimensions={0} | all-to-all | bytes 6291456 | tf_op jit(solution)/shard_map/all_to_all | solution.py:13
  125.2 0.4 copy.13
  125.5 0.0 copy-done.1
  125.5 9.3 %convert_bitcast_fusion = bf16[192,12,1024]{2,0,1:T(8,128)(2,1)} fusion(f32[12,64,1024]{2,1,0:T(8,128)S(1)} %bitcast.24, f32[192,64]{0,1:T(8,128)S(1)} %copy-done.1), kind=kOutput, calls=%fused_computation | convolution fusion | flops 1814298624 | bytes 7913472 | tf_op jit(solution)/shard_map/ma,nac->mnc/dot_general | solution.py:39
  (1 shorter events, 0.0 us)
Async XLA Ops:
  0.0 0.9 copy-start
  0.0 16.1 %copy-start.2 = (f32[768,16]{0,1:T(8,128)S(1)}, f32[768,16]{0,1:T(8,128)}, u32[]{:S(2)}) copy-start(f32[768,16]{0,1:T(8,128)} %param.7) | copy-start | bytes 147460
  81.5 44.0 %copy-start.1 = (f32[192,64]{0,1:T(8,128)S(1)}, f32[192,64]{0,1:T(8,128)}, u32[]{:S(2)}) copy-start(f32[192,64]{0,1:T(8,128)} %param.6) | copy-start | bytes 147460
